TPU v7x, 512 devices: a whole 4x8x8 slice. The times are simulated.
512 devices in a mesh: sec: 2 (over core), ctx: 64 (over x, z_hi, y), head: 4 (over z_lo).
Axes of the slice: x: 4, y: 8, z: 8 (z_hi: 2, z_lo: 4; z = z_hi * 4 + z_lo), core: 2. Of those that a mesh axis runs over, the one named last changes fastest.
Arguments:
- query_self: bfloat16 [12288, 2048], P('ctx', ('sec', 'head')), may hold values from -12 to 12
- key_self: bfloat16 [12288, 2048], P('ctx', ('sec', 'head')), may hold values from -6 to 6
- value_self: bfloat16 [12288, 2048], P('ctx', ('sec', 'head')), may hold values from -6 to 6
- query_cross: bfloat16 [12288, 2048], P('ctx', ('sec', 'head')), may hold values from -12 to 12
- neighbour_kv: bfloat16 [512, 128, 4096], P(('sec', 'ctx', 'head')), may hold values from -6 to 6
- neighbour_map: int32 [192, 2], P('ctx'), may hold values from 0 to 7, all different within a row
Outputs:
- self_out: bfloat16 [12288, 2048], P('ctx', ('sec', 'head'))
- cross_out: bfloat16 [12288, 2048], P('ctx', ('sec', 'head'))
Inputs may be any that keep to these rules, and one draw needn't show every extreme that they name: `neighbour_map`: entry v of stretch c names slot v % 1 of the device at index v // 1 along sec+head that shares stretch c's context shard; a stretch's two entries differ.
All inputs are finite; a program needn't handle non-finite values.
Results may differ from a plain program's by a relative error of at most 0.0035.
Values may be sent and summed in bfloat16 or wider, within the bound.
No kernel may reach another device: no remote copies, remote signals or barrier semaphores. Data moves between devices by JAX's collectives and lax.ppermute only.
A program may use at most 64 MiB of HBM per device.

v0:
```python
import math
import jax
import jax.numpy as jnp
from jax import lax
from jax.sharding import PartitionSpec as P

HD = 128
STRETCH = 64
MASKED_SCORE = -1e30


def attend_block(carried, queries, key_block, value_block, key_mask, score_scale):
    row_top, row_total, summed = carried
    scores = (
        jnp.einsum("qhd,khd->hqk", queries, key_block, preferred_element_type=jnp.float32)
        * score_scale
    )
    masked = jnp.where(key_mask, scores, MASKED_SCORE)
    new_top = jnp.maximum(row_top, jnp.max(masked, axis=-1))
    exp_scores = jnp.where(key_mask, jnp.exp(masked - new_top[:, :, None]), 0.0)
    factor = jnp.exp(row_top - new_top)
    row_total = row_total * factor + jnp.sum(exp_scores, axis=-1)
    update = jnp.einsum(
        "hqk,khd->qhd",
        exp_scores.astype(jnp.bfloat16),
        value_block,
        preferred_element_type=jnp.float32,
    )
    summed = summed * jnp.transpose(factor)[:, :, None] + update
    return (new_top, row_total, summed)


def attend_keys(carried, queries, key_rows, value_rows, positions, score_scale):
    key_count = key_rows.shape[0]
    head_count = queries.shape[1]
    block_rows = math.gcd(key_count, 1024)
    blocks = key_count // block_rows
    key_stack = key_rows.reshape(blocks, block_rows, head_count, HD)
    value_stack = value_rows.reshape(blocks, block_rows, head_count, HD)

    def fold_step(state_now, scanned):
        number, key_block, value_block = scanned
        places = number * block_rows + jnp.arange(block_rows, dtype=jnp.int32)
        key_mask = (places[None, None, :] <= positions[None, :, None]) & (
            places[None, None, :] >= 0
        )
        return (
            attend_block(state_now, queries, key_block, value_block, key_mask, score_scale),
            None,
        )

    carried, _ = lax.scan(
        fold_step, carried, (jnp.arange(blocks, dtype=jnp.int32), key_stack, value_stack)
    )
    return carried


def self_attention(query_self, key_self, value_self, score_scale):
    local_rows, local_width = query_self.shape
    head_count = local_width // HD
    queries = query_self.reshape(local_rows, head_count, HD)
    first_row = lax.axis_index("ctx") * local_rows
    positions = first_row + jnp.arange(local_rows, dtype=jnp.int32)
    carried = (
        jnp.full((head_count, local_rows), MASKED_SCORE, jnp.float32),
        jnp.zeros((head_count, local_rows), jnp.float32),
        jnp.zeros((local_rows, head_count, HD), jnp.float32),
    )
    carried = attend_keys(
        carried,
        queries,
        lax.all_gather(key_self, "ctx", axis=0, tiled=True),
        lax.all_gather(value_self, "ctx", axis=0, tiled=True),
        positions,
        score_scale,
    )
    row_top, row_total, summed = carried
    attended = summed / jnp.transpose(row_total)[:, :, None]
    return attended.reshape(local_rows, local_width).astype(jnp.bfloat16)


def cross_attention(query_cross, neighbour_kv, neighbour_map, score_scale):
    local_rows, local_width = query_cross.shape
    head_count = local_width // HD
    stretch_count = local_rows // STRETCH
    slot_count, block_len, features = neighbour_kv.shape
    group_count = features // (2 * local_width)
    stretch_first = lax.axis_index("ctx") * stretch_count
    keep_stretch = stretch_first + jnp.arange(stretch_count, dtype=jnp.int32) > 0
    parted = neighbour_kv.reshape(slot_count, block_len, group_count, 2 * local_width)
    received = lax.all_to_all(parted, ("sec", "head"), split_axis=2, concat_axis=0, tiled=True)
    received = received.reshape(group_count * slot_count, block_len, 2, head_count, HD)
    chosen = received[neighbour_map]
    chosen = chosen.reshape(stretch_count, neighbour_map.shape[1] * block_len, 2, head_count, HD)
    stretch_queries = query_cross.reshape(stretch_count, STRETCH, head_count, HD)
    scores = (
        jnp.einsum(
            "cqhd,ckhd->chqk", stretch_queries, chosen[:, :, 0], preferred_element_type=jnp.float32
        )
        * score_scale
    )
    row_top = jnp.max(scores, axis=-1, keepdims=True)
    exp_scores = jnp.exp(scores - row_top)
    row_total = jnp.sum(exp_scores, axis=-1)
    summed = jnp.einsum(
        "chqk,ckhd->cqhd",
        exp_scores.astype(jnp.bfloat16),
        chosen[:, :, 1],
        preferred_element_type=jnp.float32,
    )
    attended = summed / jnp.transpose(row_total, (0, 2, 1))[:, :, :, None]
    attended = attended.reshape(local_rows, local_width)
    keep_rows = jnp.repeat(keep_stretch, STRETCH)
    return jnp.where(keep_rows[:, None], attended, 0.0).astype(jnp.bfloat16)


def on_device(query_self, key_self, value_self, query_cross, neighbour_kv, neighbour_map):
    score_scale = 1.0 / math.sqrt(HD)
    self_out = self_attention(query_self, key_self, value_self, score_scale)
    cross_out = cross_attention(query_cross, neighbour_kv, neighbour_map, score_scale)
    return (self_out, cross_out)


def solution(mesh):
    return jax.shard_map(
        on_device,
        mesh=mesh,
        in_specs=(
            P("ctx", ("sec", "head")),
            P("ctx", ("sec", "head")),
            P("ctx", ("sec", "head")),
            P("ctx", ("sec", "head")),
            P(("sec", "ctx", "head"), None, None),
            P("ctx", None),
        ),
        out_specs=(P("ctx", ("sec", "head")), P("ctx", ("sec", "head"))),
        check_vma=False,
    )
```

profile of v0, /device:TPU:4, one launch (start us, length us, event | category | flops | bytes accessed | tf_op | source)
XLA Modules:
  0.0 453.8 jit_solution(10406228715060818741)
XLA Ops:
  8.0 0.7 all-gather.5.cloned.1.call-update
  8.7 2.3 copy.37
  10.9 7.4 %all-to-all-start = ((bf16[1,128,8,512]{1,3,0,2:T(8,128)(2,1)}), bf16[1,128,8,512]{1,3,0,2:T(8,128)(2,1)S(1)}, u32[]{:S(2)}, u32[]{:S(2)}) async-start(bf16[1,128,8,512]{1,3,0,2:T(8,128)(2,1)} %bitcast.1), calls=%async_computation | async-start | bytes 2097152 | tf_op jit(solution)/shard_map/all_to_all | solution.py:91
  18.8 26.6 %all-to-all-done = bf16[1,128,8,512]{1,3,0,2:T(8,128)(2,1)S(1)} async-done(((bf16[1,128,8,512]{1,3,0,2:T(8,128)(2,1)}), bf16[1,128,8,512]{1,3,0,2:T(8,128)(2,1)S(1)}, u32[]{:S(2)}, u32[]{:S(2)}) %all-to-all-start) | async-done | bytes 1048608 | tf_op jit(solution)/shard_map/all_to_all | solution.py:91
  46.1 0.7 gather_fusion
  47.9 0.7 fusion.18
  48.6 150.6 %all-gather.3.cloned.1.call-done = bf16[12288,256]{1,0:T(8,128)(2,1)} async-done(((bf16[192,256]{1,0:T(8,128)(2,1)}), bf16[12288,256]{1,0:T(8,128)(2,1)}) %all-gather.3.cloned.1.call-update) | async-done | bytes 6291472 | tf_op jit(solution)/shard_map/all_gather | solution.py:72
  199.2 9.7 %reshape.96 = bf16[12,1024,2,128]{3,2,1,0:T(2,128)(2,1)} reshape(bf16[12288,256]{1,0:T(8,128)(2,1)} %all-gather.3.cloned.1.call-done) | data formatting | bytes 12582912 | tf_op jit(solution)/shard_map/reshape | solution.py:38
  208.8 167.1 %all-gather.5.cloned.1.call-done = bf16[12288,256]{1,0:T(8,128)(2,1)} async-done(((bf16[192,256]{1,0:T(8,128)(2,1)}), bf16[12288,256]{1,0:T(8,128)(2,1)}) %all-gather.5.cloned.1.call-update) | async-done | bytes 6291472 | tf_op jit(solution)/shard_map/all_gather | solution.py:73
  375.9 9.7 %reshape.98 = bf16[12,1024,2,128]{3,2,1,0:T(2,128)(2,1)} reshape(bf16[12288,256]{1,0:T(8,128)(2,1)} %all-gather.5.cloned.1.call-done) | data formatting | bytes 12582912 | tf_op jit(solution)/shard_map/reshape | solution.py:39
  385.6 60.6 %while.15 = (s32[]{:T(128)}, f32[2,192]{1,0:T(2,128)S(1)}, f32[2,192]{1,0:T(2,128)S(1)}, f32[192,2,128]{2,0,1:T(8,128)S(1)}, s32[12]{0:T(128)S(1)}, /*index=5*/b...) while((s32[]{:T(128)}, f32[2,192]{1,0:T(2,128)S(1)}, ...), condition=%wide.region_3.4_spmd.clone, body=%wide.region_0.3_spmd.clone.sunk | while | flops 205411776 | bytes 9178801 | solution.py:52
  387.0 1.9 constant_dynamic-slice_fusion.3
  392.0 1.9 constant_dynamic-slice_fusion.3
  397.1 1.9 constant_dynamic-slice_fusion.3
  402.1 1.9 constant_dynamic-slice_fusion.3
  407.2 1.9 constant_dynamic-slice_fusion.3
  412.2 1.9 constant_dynamic-slice_fusion.3
  417.3 1.9 constant_dynamic-slice_fusion.3
  422.3 1.9 constant_dynamic-slice_fusion.3
  427.4 1.9 constant_dynamic-slice_fusion.3
  432.4 1.9 constant_dynamic-slice_fusion.3
  437.5 1.9 constant_dynamic-slice_fusion.3
  442.5 1.9 constant_dynamic-slice_fusion.3
  446.2 0.8 copy_bitcast_fusion.8
  (161 shorter events, 32.8 us)
Async XLA Ops:
  7.2 11.6 %copy-start = (bf16[192,256]{1,0:T(8,128)(2,1)S(1)}, bf16[192,256]{1,0:T(8,128)(2,1)}, u32[]{:S(2)}) copy-start(bf16[192,256]{1,0:T(8,128)(2,1)} %param.8) | copy-start | bytes 294916
  7.2 192.0 %all-gather.3.cloned.1.call-start = ((), (), s32[]{:S(2)}) async-start(), calls=%async_computation.1 | async-start | bytes 6389760 | tf_op jit(solution)/shard_map/all_gather | solution.py:72
  7.9 368.0 %all-gather.5.cloned.1.call-start = ((), (), s32[]{:S(2)}) async-start(), calls=%async_computation.2 | async-start | bytes 6389760 | tf_op jit(solution)/shard_map/all_gather | solution.py:73
  10.9 7.6 %copy-start.2 = (s32[3,2]{0,1:T(2,128)S(1)}, s32[3,2]{0,1:T(2,128)}, u32[]{:S(2)}) copy-start(s32[3,2]{0,1:T(2,128)} %param.13) | copy-start | bytes 76
  10.9 7.8 %copy-start.1 = (bf16[192,256]{1,0:T(8,128)(2,1)S(1)}, bf16[192,256]{1,0:T(8,128)(2,1)}, u32[]{:S(2)}) copy-start(bf16[192,256]{1,0:T(8,128)(2,1)} %param.11) | copy-start | bytes 294916
  10.9 34.5 %all-to-all-start = ((bf16[1,128,8,512]{1,3,0,2:T(8,128)(2,1)}), bf16[1,128,8,512]{1,3,0,2:T(8,128)(2,1)S(1)}, u32[]{:S(2)}, u32[]{:S(2)}) async-start(bf16[1,128,8,512]{1,3,0,2:T(8,128)(2,1)} %bitcast.1), calls=%async_computation | async-start | bytes 2097152 | tf_op jit(solution)/shard_map/all_to_all | solution.py:91
Sparse Core Ops, SparseCore 0:
  12.4 186.6 all-gather.2
  203.6 172.2 all-gather.4
where the time goes:
time: 455 us; the launch traced here: 454 us
  waiting for transfers between devices  346 us (76%)
  local copies, waits for them, and re-layouts  53.5 us (12%)
  matrix products  14.5 us (3%)
  between operations  14.2 us (3%)
  other arithmetic  11.1 us (2%)
  loops' own time  7.49 us (2%)
  starting transfers between devices  7.47 us (2%)
    all_gather x1, waiting for transfers between devices, self_attention(): lax.all_gather(value_self, 'ctx', axis=0, tiled=True)  167 us
    all_gather x1, waiting for transfers between devices, self_attention(): lax.all_gather(key_self, 'ctx', axis=0, tiled=True)  151 us
    dynamic_slice x24, local copies, waits for them, and re-layouts, attend_keys(): lax.scan(fold_step, carried, (jnp.arange(blocks, dtype=jnp.int32), key_st...  29.8 us
    all_to_all x1, waiting for transfers between devices, cross_attention(): lax.all_to_all(parted, ('sec', 'head'), split_axis=2, concat_axis=0, tile...  26.6 us
    reshape x1, local copies, waits for them, and re-layouts, attend_keys(): value_stack = value_rows.reshape(blocks, block_rows, head_count, HD)  9.73 us
    reshape x1, local copies, waits for them, and re-layouts, attend_keys(): key_stack = key_rows.reshape(blocks, block_rows, head_count, HD)  9.69 us
  transfers between devices with their start and end apart: 3, of which 3 were waited for; matrix products, arithmetic and copies ran while one was open for 3% of the time, Pallas kernels for 0%

commit v1 on v0

--- a/solution.py
+++ b/solution.py
@@ -70,7 +70,9 @@
         carried,
         queries,
         lax.all_gather(key_self, "ctx", axis=0, tiled=True),
-        lax.all_gather(value_self, "ctx", axis=0, tiled=True),
+        jnp.concatenate(
+            lax.all_to_all(jnp.stack([value_self] * lax.axis_size("ctx")), "ctx", 0, 0), axis=0
+        ),
         positions,
         score_scale,
     )

time: 455 us -> 423 us (0.930)
  waiting for transfers between devices: 346 us -> 267 us
  blocking collectives: 0 us -> 33.4 us
  starting transfers between devices: 7.47 us -> 16.8 us
    all_gather x1 -> x0, waiting for transfers between devices: 167 us -> none  [self_attention(): lax.all_gather(value_self, 'ctx', axis=0, tiled=True)]
    all_to_all x1, waiting for transfers between devices: 26.6 us -> 146 us  [self_attention(): lax.all_to_all(jnp.stack([value_self] * lax.axis_size('ctx')), 'ctx', 0, 0)]
    all_to_all x0 -> x1, blocking collectives: none -> 33.4 us  [cross_attention(): lax.all_to_all(parted, ('sec', 'head'), split_axis=2, concat_axis=0, tile...]
    all_gather x1, waiting for transfers between devices: 151 us -> 121 us  [self_attention(): lax.all_gather(key_self, 'ctx', axis=0, tiled=True)]
    another operation x0 -> x2, local copies, waits for them, and re-layouts: none -> 13.2 us  [the longest x1 9.78 us: attend_keys(): value_stack = value_rows.reshape(blocks, block_rows, head_count, HD)]
    reshape x1 -> x0, local copies, waits for them, and re-layouts: 9.73 us -> none  [attend_keys(): value_stack = value_rows.reshape(blocks, block_rows, head_count, HD)]
    all_to_all x1, starting transfers between devices: 7.4 us -> 16.8 us  [self_attention(): lax.all_to_all(jnp.stack([value_self] * lax.axis_size('ctx')), 'ctx', 0, 0)]
  transfers between devices with their start and end apart: 3 -> 2, of which waited for: 3 -> 2; matrix products, arithmetic and copies ran while one was open for 3% -> 3% of each run, Pallas kernels for 0% -> 0%
where the time goes in v1:
time: 423 us; the launch traced here: 422 us
  waiting for transfers between devices  267 us (63%)
  local copies, waits for them, and re-layouts  57.1 us (13%)
  blocking collectives  33.4 us (8%)
  starting transfers between devices  16.8 us (4%)
  matrix products  14.2 us (3%)
  between operations  14.2 us (3%)
  other arithmetic  10.9 us (3%)
  loops' own time  8.51 us (2%)
    all_to_all x1, waiting for transfers between devices, self_attention(): lax.all_to_all(jnp.stack([value_self] * lax.axis_size('ctx')), 'ctx', 0, 0)  146 us
    all_gather x1, waiting for transfers between devices, self_attention(): lax.all_gather(key_self, 'ctx', axis=0, tiled=True)  121 us
    all_to_all x1, blocking collectives, cross_attention(): lax.all_to_all(parted, ('sec', 'head'), split_axis=2, concat_axis=0, tile...  33.4 us
    dynamic_slice x24, local copies, waits for them, and re-layouts, attend_keys(): lax.scan(fold_step, carried, (jnp.arange(blocks, dtype=jnp.int32), key_st...  30.6 us
    all_to_all x1, starting transfers between devices, self_attention(): lax.all_to_all(jnp.stack([value_self] * lax.axis_size('ctx')), 'ctx', 0, 0)  16.8 us
    another operation x1, local copies, waits for them, and re-layouts, attend_keys(): value_stack = value_rows.reshape(blocks, block_rows, head_count, HD)  9.78 us
    reshape x1, local copies, waits for them, and re-layouts, attend_keys(): key_stack = key_rows.reshape(blocks, block_rows, head_count, HD)  9.72 us
    another operation x1, loops' own time, attend_keys(): lax.scan(fold_step, carried, (jnp.arange(blocks, dtype=jnp.int32), key_st...  8.51 us
  transfers between devices with their start and end apart: 2, of which 2 were waited for; matrix products, arithmetic and copies ran while one was open for 3% of the time, Pallas kernels for 0%

profile of v1, /device:TPU:4, one launch (start us, length us, event | category | flops | bytes accessed | tf_op | source)
XLA Modules:
  0.0 422.3 jit_solution(8643528946486859085)
XLA Ops:
  7.2 1.6 copy.37
  8.8 33.4 %all_to_all.20 = bf16[1,128,8,512]{1,3,0,2:T(8,128)(2,1)S(1)} all-to-all(bf16[1,128,8,512]{1,3,0,2:T(8,128)(2,1)S(1)} %bitcast.70), channel_id=1, replica_groups=mesh['sec'=2,'ctx'=64,'head'=4] {'sec','head'}, dimensions={2} | all-to-all | bytes 2097152 | tf_op jit(solution)/shard_map/all_to_all | solution.py:93
  42.3 3.4 stack.2
  45.7 16.8 %all-to-all-start = ((bf16[64,192,256]{2,1,0:T(8,128)(2,1)}), bf16[64,192,256]{2,1,0:T(8,128)(2,1)}, u32[]{:S(2)}, u32[]{:S(2)}) async-start(bf16[64,192,256]{2,1,0:T(8,128)(2,1)} %stack.2), calls=%async_computation | async-start | bytes 12582912 | tf_op jit(solution)/shard_map/all_to_all | solution.py:74
  64.3 0.7 gather_fusion
  66.1 0.7 fusion.18
  66.8 145.7 %all-to-all-done = bf16[64,192,256]{2,1,0:T(8,128)(2,1)} async-done(((bf16[64,192,256]{2,1,0:T(8,128)(2,1)}), bf16[64,192,256]{2,1,0:T(8,128)(2,1)}, u32[]{:S(2)}, u32[]{:S(2)}) %all-to-all-start) | async-done | bytes 6291488 | tf_op jit(solution)/shard_map/all_to_all | solution.py:74
  212.5 9.8 %reshape_reshape.3 = bf16[12,1024,2,128]{3,2,1,0:T(2,128)(2,1)} reshape(bf16[64,192,256]{2,1,0:T(8,128)(2,1)} %all-to-all-done) | data formatting | bytes 12582912 | tf_op jit(solution)/shard_map/reshape;reshape | solution.py:39
  222.3 120.8 %all-gather.2.cloned.1.call-done = bf16[12288,256]{1,0:T(8,128)(2,1)} async-done(((bf16[192,256]{1,0:T(8,128)(2,1)}), bf16[12288,256]{1,0:T(8,128)(2,1)}) %all-gather.2.cloned.1.call-update) | async-done | bytes 6291472 | tf_op jit(solution)/shard_map/all_gather | solution.py:72
  343.1 9.7 %reshape.95 = bf16[12,1024,2,128]{3,2,1,0:T(2,128)(2,1)} reshape(bf16[12288,256]{1,0:T(8,128)(2,1)} %all-gather.2.cloned.1.call-done) | data formatting | bytes 12582912 | tf_op jit(solution)/shard_map/reshape | solution.py:38
  352.8 61.8 %while.15 = (s32[]{:T(128)}, f32[2,192]{1,0:T(2,128)S(1)}, f32[2,192]{1,0:T(2,128)S(1)}, f32[192,2,128]{2,0,1:T(8,128)S(1)}, s32[12]{0:T(128)S(1)}, /*index=5*/b...) while((s32[]{:T(128)}, f32[2,192]{1,0:T(2,128)S(1)}, ...), condition=%wide.region_3.4_spmd.clone, body=%wide.region_0.3_spmd.clone.sunk | while | flops 205411776 | bytes 9178793 | solution.py:52
  354.3 1.9 constant_dynamic-slice_fusion.3
  359.5 1.9 constant_dynamic-slice_fusion.3
  364.6 1.9 constant_dynamic-slice_fusion.3
  369.8 1.9 constant_dynamic-slice_fusion.3
  374.9 1.9 constant_dynamic-slice_fusion.3
  380.1 1.9 constant_dynamic-slice_fusion.3
  385.3 1.9 constant_dynamic-slice_fusion.3
  390.4 1.9 constant_dynamic-slice_fusion.3
  395.6 1.9 constant_dynamic-slice_fusion.3
  400.7 1.9 constant_dynamic-slice_fusion.3
  405.9 1.9 constant_dynamic-slice_fusion.3
  411.0 1.9 constant_dynamic-slice_fusion.3
  414.7 0.8 copy_bitcast_fusion.8
  (162 shorter events, 33.0 us)
Async XLA Ops:
  7.2 56.5 %copy-start = (bf16[192,256]{1,0:T(8,128)(2,1)S(1)}, bf16[192,256]{1,0:T(8,128)(2,1)}, u32[]{:S(2)}) copy-start(bf16[192,256]{1,0:T(8,128)(2,1)} %param.8) | copy-start | bytes 294916
  8.8 33.4 %copy-start.2 = (bf16[192,256]{1,0:T(8,128)(2,1)S(1)}, bf16[192,256]{1,0:T(8,128)(2,1)}, u32[]{:S(2)}) copy-start(bf16[192,256]{1,0:T(8,128)(2,1)} %param.10) | copy-start | bytes 294916
  45.7 17.5 %copy-start.3 = (s32[3,2]{0,1:T(2,128)S(1)}, s32[3,2]{0,1:T(2,128)}, u32[]{:S(2)}) copy-start(s32[3,2]{0,1:T(2,128)} %param.13) | copy-start | bytes 76
  45.7 17.7 %copy-start.1 = (bf16[192,256]{1,0:T(8,128)(2,1)S(1)}, bf16[192,256]{1,0:T(8,128)(2,1)}, u32[]{:S(2)}) copy-start(bf16[192,256]{1,0:T(8,128)(2,1)} %param.11) | copy-start | bytes 294916
  45.7 166.9 %all-to-all-start = ((bf16[64,192,256]{2,1,0:T(8,128)(2,1)}), bf16[64,192,256]{2,1,0:T(8,128)(2,1)}, u32[]{:S(2)}, u32[]{:S(2)}) async-start(bf16[64,192,256]{2,1,0:T(8,128)(2,1)} %stack.2), calls=%async_computation | async-start | bytes 12582912 | tf_op jit(solution)/shard_map/all_to_all | solution.py:74
  62.4 280.7 %all-gather.2.cloned.1.call-start = ((), (), s32[]{:S(2)}) async-start(), calls=%async_computation.2 | async-start | bytes 6389760 | tf_op jit(solution)/shard_map/all_gather | solution.py:72
Sparse Core Ops, SparseCore 0:
  67.7 275.3 all-gather.1
